TPU v7x, 32 devices: a whole 2x2x4 slice. The times are simulated.
32 devices in a mesh: dp: 2 (over core), ctx: 4 (over y, x), tp: 4 (over z).
Axes of the slice: x: 2, y: 2, z: 4, core: 2. Of those that a mesh axis runs over, the one named last changes fastest.
Arguments:
- queries: bfloat16 [4, 8192, 1536], P('dp', 'tp', 'ctx'), may hold values from -6 to 6
- key_proj: bfloat16 [4, 8192, 1536], P('dp', 'tp', 'ctx'), may hold values from -6 to 6
- value_proj: bfloat16 [4, 8192, 1536], P('dp', 'tp', 'ctx'), may hold values from -6 to 6
- grad_output: bfloat16 [4, 8192, 1536], P('dp', 'tp', 'ctx'), may hold values from -6 to 6
- filters: float32 [512, 128], P('tp'), may hold values from -0.5 to 0.5
- group_of: int32 [8192], P('tp'), may hold values from 0 to 511, as said below
Outputs:
- gated_out: bfloat16 [4, 8192, 1536], P('dp', 'tp', 'ctx')
- grad_queries: bfloat16 [4, 8192, 1536], P('dp', 'tp', 'ctx')
- grad_keys: bfloat16 [4, 8192, 1536], P('dp', 'tp', 'ctx')
- grad_values: bfloat16 [4, 8192, 1536], P('dp', 'tp', 'ctx')
- grad_filters: float32 [512, 128], P('tp')
Inputs may be any that keep to these rules, and one draw needn't show every extreme that they name: `group_of`: channels come in aligned runs of 16 consecutive channels that share one filter row, and every filter row serves exactly one run.
All inputs are finite; a program needn't handle non-finite values.
Results may differ from a plain program's by a relative error of at most 0.0058.
Values may be sent and summed in bfloat16 or wider, within the bound.
No kernel may reach another device: no remote copies, remote signals or barrier semaphores. Data moves between devices by JAX's collectives and lax.ppermute only.
A program may use at most 192 MiB of HBM per device.

v0:
```python
import jax
import jax.numpy as jnp
from jax import lax
from jax.sharding import PartitionSpec as P

D = 8192
GROUPS = 512


def passed_along(block, axis, distance):
    devices = range(lax.axis_size(axis))
    route = [(i - distance, i) for i in devices if i - distance in devices]
    return lax.ppermute(block, axis, route)


def band_apply(matrix, rows_in, block_rows, groups_here):
    channels, positions = rows_in.shape
    blocked = rows_in.reshape(
        groups_here, channels // groups_here, positions // block_rows, block_rows
    )
    result = jnp.einsum("rmbj,rij->rmbi", blocked, matrix, preferred_element_type=jnp.float32)
    return result.reshape(channels, positions)


def band_adjoint(matrix, rows_in, block_rows, groups_here):
    channels, positions = rows_in.shape
    blocked = rows_in.reshape(
        groups_here, channels // groups_here, positions // block_rows, block_rows
    )
    result = jnp.einsum("rmbj,rji->rmbi", blocked, matrix, preferred_element_type=jnp.float32)
    return result.reshape(channels, positions)


def band_outer(left_rows, right_rows, block_rows, groups_here):
    channels, positions = left_rows.shape
    shape_four = (groups_here, channels // groups_here, positions // block_rows, block_rows)
    return jnp.einsum(
        "rmbi,rmbj->rij",
        left_rows.reshape(shape_four),
        right_rows.reshape(shape_four),
        preferred_element_type=jnp.float32,
    )


def shards(queries, key_proj, value_proj, grad_output, filters, group_of):
    wide = jnp.float32
    windows, channels, positions = queries.shape
    block_rows = filters.shape[1]
    members = D // GROUPS
    groups_here = channels // members
    filter_table = lax.all_gather(filters.astype(jnp.bfloat16), "tp", axis=0, tiled=True)
    run_group = group_of.reshape(groups_here, members)[:, 0]
    selector = (run_group[:, None] == jnp.arange(GROUPS, dtype=jnp.int32)[None, :]).astype(
        jnp.bfloat16
    )
    run_filters = jnp.dot(selector, filter_table, preferred_element_type=wide).astype(jnp.bfloat16)
    template = jnp.concatenate(
        [
            jnp.zeros((groups_here, 1), jnp.bfloat16),
            run_filters[:, ::-1],
            jnp.zeros((groups_here, block_rows), jnp.bfloat16),
        ],
        axis=1,
    )
    toeplitz = jnp.tile(template, (1, block_rows))[:, : 2 * block_rows * block_rows]
    toeplitz = toeplitz.reshape(groups_here, block_rows, 2 * block_rows)
    lower_band = toeplitz[:, :, :block_rows]
    upper_band = toeplitz[:, :, block_rows:]
    product = (key_proj.astype(wide) * value_proj.astype(wide)).astype(jnp.bfloat16)
    before = passed_along(product[:, :, -block_rows:], "ctx", 1)
    backward = (grad_output.astype(wide) * queries.astype(wide)).astype(jnp.bfloat16)
    after = passed_along(backward[:, :, :block_rows], "ctx", -1)
    gated_list = []
    gradq_list = []
    gradk_list = []
    gradv_list = []
    outer_total = jnp.zeros((groups_here, block_rows, 2 * block_rows), wide)
    for window in range(windows):
        product_w = product[window]
        backward_w = backward[window]
        previous = jnp.concatenate([before[window], product_w[:, :-block_rows]], axis=1)
        following = jnp.concatenate([backward_w[:, block_rows:], after[window]], axis=1)
        mixed_rows = band_apply(upper_band, product_w, block_rows, groups_here)
        mixed_rows = mixed_rows + band_apply(lower_band, previous, block_rows, groups_here)
        gated_list.append((queries[window].astype(wide) * mixed_rows).astype(jnp.bfloat16))
        gradq_list.append((grad_output[window].astype(wide) * mixed_rows).astype(jnp.bfloat16))
        upward = band_adjoint(upper_band, backward_w, block_rows, groups_here)
        upward = upward + band_adjoint(lower_band, following, block_rows, groups_here)
        gradk_list.append((upward * value_proj[window].astype(wide)).astype(jnp.bfloat16))
        gradv_list.append((upward * key_proj[window].astype(wide)).astype(jnp.bfloat16))
        outer_total = outer_total + jnp.concatenate(
            [
                band_outer(backward_w, previous, block_rows, groups_here),
                band_outer(backward_w, product_w, block_rows, groups_here),
            ],
            axis=2,
        )
    gated_out = jnp.stack(gated_list, axis=0)
    grad_queries = jnp.stack(gradq_list, axis=0)
    grad_keys = jnp.stack(gradk_list, axis=0)
    grad_values = jnp.stack(gradv_list, axis=0)
    flattened = outer_total.reshape(groups_here, 2 * block_rows * block_rows)
    flattened = jnp.pad(flattened, ((0, 0), (0, block_rows)))
    diagonals = jnp.sum(flattened.reshape(groups_here, block_rows, 2 * block_rows + 1), axis=1)
    run_grad = diagonals[:, block_rows:0:-1]
    scale_by = 1.0 / (windows * positions * lax.axis_size("dp") * lax.axis_size("ctx"))
    table_grad = (
        jnp.dot(selector.astype(wide).T, run_grad, precision=lax.Precision.HIGHEST) * scale_by
    )
    whole_grad = lax.psum(table_grad, ("dp", "ctx"))
    grad_filters = lax.psum_scatter(whole_grad, "tp", scatter_dimension=0, tiled=True)
    return (gated_out, grad_queries, grad_keys, grad_values, grad_filters)


def solution(mesh):
    in_specs = (
        P("dp", "tp", "ctx"),
        P("dp", "tp", "ctx"),
        P("dp", "tp", "ctx"),
        P("dp", "tp", "ctx"),
        P("tp", None),
        P("tp"),
    )
    out_specs = (
        P("dp", "tp", "ctx"),
        P("dp", "tp", "ctx"),
        P("dp", "tp", "ctx"),
        P("dp", "tp", "ctx"),
        P("tp", None),
    )
    return jax.shard_map(shards, mesh=mesh, in_specs=in_specs, out_specs=out_specs, check_vma=False)
```

profile of v0, /device:TPU:0, one launch (start us, length us, event | category | flops | bytes accessed | tf_op | source)
XLA Modules:
  0.0 380.6 jit_solution(17023830327281348778)
XLA Ops:
  15.3 6.5 %collective-permute-start = (bf16[2,2048,128]{2,1,0:T(8,128)(2,1)}, bf16[2,2048,128]{2,1,0:T(8,128)(2,1)}, u32[]{:S(2)}, u32[]{:S(2)}) collective-permute-start(bf16[2,2048,128]{2,1,0:T(8,128)(2,1)} %slice.112), channel_id=1, source_target_pairs={{0,4},{4,8},{8,12},{1,5},{5,9},{9,13},{2,6},{6,10},{10,14},{3,7},{... | collective-permute-start | bytes 3145736 | tf_op jit(solution)/shard_map/ppermute | solution.py:13
  24.8 14.4 %all_gather.3 = bf16[512,128]{1,0:T(8,128)(2,1)S(1)} all-gather(bf16[128,128]{1,0:T(8,128)(2,1)S(1)} %convert_element_type.96), channel_id=1, replica_groups=mesh['dp'=2,'ctx'=4,'tp'=4] {'tp'}, dimensions={0}, use_global_device_ids=true | all-gather | bytes 163840 | tf_op jit(solution)/shard_map/all_gather | solution.py:51
  44.3 12.9 %tile.10 = bf16[128,32896]{0,1:T(8,128)(2,1)} reshape(bf16[128,128,257]{0,2,1:T(8,128)(2,1)} %tile.4) | data formatting | bytes 16842752 | tf_op jit(solution)/shard_map/tile | solution.py:65
  64.4 6.7 %copy.88 = bf16[128,128,128]{2,1,0:T(8,128)(2,1)} copy(bf16[128,128,128]{0,2,1:T(8,128)(2,1)} %get-tuple-element.6) | data formatting | bytes 8388608
  73.1 6.7 %copy.87 = bf16[128,128,128]{2,1,0:T(8,128)(2,1)} copy(bf16[128,128,128]{0,2,1:T(8,128)(2,1)} %get-tuple-element.5) | data formatting | bytes 8388608
  95.1 5.2 %reshape_squeeze.8 = bf16[128,16,3,128]{3,2,1,0:T(4,128)(2,1)} reshape(bf16[1,2048,384]{2,1,0:T(8,128)(2,1)} %get-tuple-element.19) | data formatting | bytes 3145728 | tf_op jit(solution)/shard_map/reshape;squeeze | solution.py:18
  100.3 6.3 %convolution_bitcast_fusion = f32[128,128,128]{1,2,0:T(8,128)} fusion(bf16[128,16,3,128]{3,2,1,0:T(4,128)(2,1)} %reshape_squeeze.9, bf16[128,16,3,128]{3,2,1,0:T(4,128)(2,1)S(1)} %reshape_squeeze.21), kind=kOutput, calls=%fused_computation.19 | convolution fusion | flops 201326592 | bytes 11534336 | tf_op jit(solution)/shard_map/rmbi,rmbj->rij/dot_general | solution.py:37
  119.7 5.6 %reshape.131 = bf16[128,16,3,128]{3,2,1,0:T(4,128)(2,1)} reshape(bf16[2048,384]{1,0:T(8,128)(2,1)} %get-tuple-element.27) | data formatting | bytes 3145728 | tf_op jit(solution)/shard_map/reshape | solution.py:18
  125.4 6.3 %convolution_bitcast_fusion.1 = f32[128,128,128]{1,2,0:T(8,128)} fusion(bf16[128,16,3,128]{3,2,1,0:T(4,128)(2,1)} %reshape.132, bf16[128,16,3,128]{3,2,1,0:T(4,128)(2,1)S(1)} %reshape_squeeze.21), kind=kOutput, calls=%fused_computation.20 | convolution fusion | flops 201326592 | bytes 11534336 | tf_op jit(solution)/shard_map/rmbi,rmbj->rij/dot_general | solution.py:37
  149.0 5.1 %reshape.133 = bf16[128,16,3,128]{3,2,1,0:T(4,128)(2,1)} reshape(bf16[2048,384]{1,0:T(8,128)(2,1)} %get-tuple-element.29) | data formatting | bytes 3145728 | tf_op jit(solution)/shard_map/reshape | solution.py:27
  163.9 6.0 %add.74 = f32[1,2048,384]{2,1,0:T(8,128)} reshape(f32[128,16,3,128]{3,2,1,0:T(4,128)} %copy.67) | data formatting | bytes 6291456 | tf_op jit(solution)/shard_map/add | solution.py:88
  169.9 5.3 %reshape.134 = bf16[128,16,3,128]{3,2,1,0:T(4,128)(2,1)} reshape(bf16[2048,384]{1,0:T(8,128)(2,1)} %get-tuple-element.30) | data formatting | bytes 3145728 | tf_op jit(solution)/shard_map/reshape | solution.py:27
  184.5 6.2 %add.76 = f32[1,2048,384]{2,1,0:T(8,128)} reshape(f32[128,16,3,128]{3,2,1,0:T(4,128)} %copy.70) | data formatting | bytes 6291456 | tf_op jit(solution)/shard_map/add | solution.py:88
  190.8 6.2 %fusion.19 = f32[128,16,3,128]{3,1,2,0:T(8,128)S(1)} fusion(f32[128,16,3,128]{3,1,2,0:T(8,128)} %fusion.4, bf16[128,128,128]{2,1,0:T(8,128)(2,1)} %copy.87, bf16[128,16,3,128]{3,2,1,0:T(4,128)(2,1)S(1)} %copy-done.9), kind=kOutput, calls=%fused_computation.36 | convolution fusion | flops 202113024 | bytes 12058624 | tf_op jit(solution)/shard_map/rmbj,rij->rmbi/dot_general | solution.py:21
  200.7 6.2 %add.72 = f32[1,2048,384]{2,1,0:T(8,128)} reshape(f32[128,16,3,128]{3,2,1,0:T(4,128)} %copy.64) | data formatting | bytes 6291456 | tf_op jit(solution)/shard_map/add | solution.py:84
  206.9 6.2 %fusion.16 = f32[128,16,3,128]{3,1,2,0:T(8,128)S(1)} fusion(f32[128,16,3,128]{3,1,2,0:T(8,128)} %fusion.6, bf16[128,128,128]{2,1,0:T(8,128)(2,1)} %copy.87, bf16[128,16,3,128]{3,2,1,0:T(4,128)(2,1)S(1)} %copy-done.8), kind=kOutput, calls=%fused_computation.35 | convolution fusion | flops 202113024 | bytes 12058624 | tf_op jit(solution)/shard_map/rmbj,rij->rmbi/dot_general | solution.py:21
  216.8 6.2 %add.70 = f32[1,2048,384]{2,1,0:T(8,128)} reshape(f32[128,16,3,128]{3,2,1,0:T(4,128)} %copy.61) | data formatting | bytes 6291456 | tf_op jit(solution)/shard_map/add | solution.py:84
  223.0 17.8 %maximum_add_fusion = f32[128,128,256]{1,2,0:T(8,128)} fusion(f32[128,128,128]{1,2,0:T(8,128)} %convolution_bitcast_fusion.2, f32[128,128,128]{1,2,0:T(8,128)} %convolution_bitcast_fusion.3, f32[128,128,128]{1,2,0:T(8,128)} %convolution_bitcast_fusion, f32[128,128,128]{1,2,0:T(8,128)} %convolution_bitcast_fusion.1), kind=kLoop, calls=%fused_computation | loop fusion | flops 12582912 | bytes 50331648 | tf_op jit(solution)/shard_map/add | solution.py:91
  240.8 17.7 %copy.79 = f32[128,128,256]{0,2,1:T(8,128)} copy(f32[128,128,256]{1,2,0:T(8,128)} %maximum_add_fusion) | data formatting | bytes 33554432 | tf_op jit(solution)/shard_map/add | solution.py:91
  258.5 13.3 %pad.4 = f32[128,32896]{0,1:T(8,128)} pad(f32[128,32768]{0,1:T(8,128)} %bitcast.67, f32[]{:T(128)} %constant.4.clone.1), padding=0_0x0_128 | pad | bytes 33619972 | tf_op jit(solution)/shard_map/jit(_pad)/pad | solution.py:103
  271.8 17.5 %reshape.135 = f32[128,128,257]{0,2,1:T(8,128)} reshape(f32[128,32896]{0,1:T(8,128)} %pad.4) | data formatting | bytes 33685504 | tf_op jit(solution)/shard_map/reshape | solution.py:104
  289.2 6.9 %reduce_sum.9 = f32[128,257]{0,1:T(8,128)S(1)} reduce(f32[128,128,257]{0,2,1:T(8,128)} %reshape.135, f32[]{:T(128)} %constant.4.clone.1), dimensions={1}, to_apply=%region_0.1 | reduce | flops 4177792 | bytes 16974340 | tf_op jit(solution)/shard_map/reduce_sum | solution.py:104
  311.6 5.9 %reduce-scatter.2.cloned.1.call-done = f32[128,128]{1,0:T(8,128)} async-done(((f32[512,128]{1,0:T(8,128)}), f32[128,128]{1,0:T(8,128)}) %reduce-scatter.2.cloned.1.call-update) | async-done | bytes 65552 | tf_op jit(solution)/shard_map/reduce_scatter | solution.py:111
  319.6 52.5 %all-reduce.3.cloned.1.call-done = f32[128,128]{1,0:T(8,128)} async-done(((f32[128,128]{1,0:T(8,128)}), f32[128,128]{1,0:T(8,128)}) %all-reduce.3.cloned.1.call-update) | async-done | bytes 65552 | tf_op jit(solution)/shard_map/psum | solution.py:110
  (109 shorter events, 116.5 us)
Async XLA Ops:
  7.2 310.4 %reduce-scatter.2.cloned.1.call-start = ((), (), s32[]{:S(2)}) async-start(), calls=%async_computation.1 | async-start | bytes 327680 | tf_op jit(solution)/shard_map/reduce_scatter | solution.py:111
  7.2 6.1 %copy-start.15 = (bf16[2,2048,384]{2,1,0:T(8,128)(2,1)S(1)}, bf16[2,2048,384]{2,1,0:T(8,128)(2,1)}, u32[]{:S(2)}) copy-start(bf16[2,2048,384]{2,1,0:T(8,128)(2,1)} %param.8) | copy-start | bytes 9437188
  7.2 6.1 %copy-start.16 = (bf16[2,2048,384]{2,1,0:T(8,128)(2,1)S(1)}, bf16[2,2048,384]{2,1,0:T(8,128)(2,1)}, u32[]{:S(2)}) copy-start(bf16[2,2048,384]{2,1,0:T(8,128)(2,1)} %param.7) | copy-start | bytes 9437188
  12.0 133.6 %collective-permute-start.1 = (bf16[2,2048,128]{2,1,0:T(8,128)(2,1)}, bf16[2,2048,128]{2,1,0:T(8,128)(2,1)}, u32[]{:S(2)}, u32[]{:S(2)}) collective-permute-start(bf16[2,2048,128]{2,1,0:T(8,128)(2,1)} %slice.121), channel_id=1, source_target_pairs={{4,0},{8,4},{12,8},{5,1},{9,5},{13,9},{6,2},{10,6},{14,10},{7,3},{... | collective-permute-start | bytes 3145736 | tf_op jit(solution)/shard_map/ppermute | solution.py:13
  14.1 9.3 %copy-start.6 = (bf16[2,2048,384]{2,1,0:T(8,128)(2,1)}, bf16[2,2048,384]{2,1,0:T(8,128)(2,1)S(1)}, u32[]{:S(2)}) copy-start(bf16[2,2048,384]{2,1,0:T(8,128)(2,1)S(1)} %multiply_convert_fusion.1) | copy-start | bytes 9437188
  15.3 95.9 %collective-permute-start = (bf16[2,2048,128]{2,1,0:T(8,128)(2,1)}, bf16[2,2048,128]{2,1,0:T(8,128)(2,1)}, u32[]{:S(2)}, u32[]{:S(2)}) collective-permute-start(bf16[2,2048,128]{2,1,0:T(8,128)(2,1)} %slice.112), channel_id=1, source_target_pairs={{0,4},{4,8},{8,12},{1,5},{5,9},{9,13},{2,6},{6,10},{10,14},{3,7},{... | collective-permute-start | bytes 3145736 | tf_op jit(solution)/shard_map/ppermute | solution.py:13
  100.3 6.3 %copy-start.3 = (bf16[128,16,3,128]{3,2,1,0:T(4,128)(2,1)S(1)}, bf16[128,16,3,128]{3,2,1,0:T(4,128)(2,1)}, u32[]{:S(2)}) copy-start(bf16[128,16,3,128]{3,2,1,0:T(4,128)(2,1)} %reshape_squeeze.20) | copy-start | bytes 4718596
  100.3 6.3 %copy-start.7 = (bf16[128,16,3,128]{3,2,1,0:T(4,128)(2,1)S(1)}, bf16[128,16,3,128]{3,2,1,0:T(4,128)(2,1)}, u32[]{:S(2)}) copy-start(bf16[128,16,3,128]{3,2,1,0:T(4,128)(2,1)} %reshape_squeeze.8) | copy-start | bytes 4718596
  106.6 5.9 %copy-start.20 = (bf16[2048,256]{1,0:T(8,128)(2,1)S(1)}, bf16[2048,256]{1,0:T(8,128)(2,1)}, u32[]{:S(2)}) copy-start(bf16[2048,256]{1,0:T(8,128)(2,1)} %slice.114) | copy-start | bytes 3145732
  106.6 5.9 %copy-start.21 = (bf16[2048,256]{1,0:T(8,128)(2,1)S(1)}, bf16[2048,256]{1,0:T(8,128)(2,1)}, u32[]{:S(2)}) copy-start(bf16[2048,256]{1,0:T(8,128)(2,1)} %slice.118) | copy-start | bytes 3145732
  125.3 6.3 %copy-start.4 = (bf16[128,16,3,128]{3,2,1,0:T(4,128)(2,1)S(1)}, bf16[128,16,3,128]{3,2,1,0:T(4,128)(2,1)}, u32[]{:S(2)}) copy-start(bf16[128,16,3,128]{3,2,1,0:T(4,128)(2,1)} %reshape_squeeze.20) | copy-start | bytes 4718596
  125.4 6.3 %copy-start.11 = (bf16[128,16,3,128]{3,2,1,0:T(4,128)(2,1)S(1)}, bf16[128,16,3,128]{3,2,1,0:T(4,128)(2,1)}, u32[]{:S(2)}) copy-start(bf16[128,16,3,128]{3,2,1,0:T(4,128)(2,1)} %reshape.131) | copy-start | bytes 4718596
  131.6 4.8 %copy-start.2 = (bf16[128,128,128]{2,1,0:T(8,128)(2,1)S(1)}, bf16[128,128,128]{2,1,0:T(8,128)(2,1)}, u32[]{:S(2)}) copy-start(bf16[128,128,128]{2,1,0:T(8,128)(2,1)} %copy.88) | copy-start | bytes 12582916
  131.6 4.8 %copy-start.10 = (bf16[128,16,3,128]{3,2,1,0:T(4,128)(2,1)S(1)}, bf16[128,16,3,128]{3,2,1,0:T(4,128)(2,1)}, u32[]{:S(2)}) copy-start(bf16[128,16,3,128]{3,2,1,0:T(4,128)(2,1)} %reshape.132) | copy-start | bytes 4718596
  141.0 5.9 %copy-start.19 = (bf16[2048,256]{1,0:T(8,128)(2,1)S(1)}, bf16[2048,256]{1,0:T(8,128)(2,1)}, u32[]{:S(2)}) copy-start(bf16[2048,256]{1,0:T(8,128)(2,1)} %slice.124) | copy-start | bytes 3145732
  154.1 4.7 %copy-start.5 = (bf16[128,16,3,128]{3,2,1,0:T(4,128)(2,1)S(1)}, bf16[128,16,3,128]{3,2,1,0:T(4,128)(2,1)}, u32[]{:S(2)}) copy-start(bf16[128,16,3,128]{3,2,1,0:T(4,128)(2,1)} %reshape_squeeze.20) | copy-start | bytes 4718596
  175.2 4.2 %copy-start.1 = (bf16[128,128,128]{2,1,0:T(8,128)(2,1)S(1)}, bf16[128,128,128]{2,1,0:T(8,128)(2,1)}, u32[]{:S(2)}) copy-start(bf16[128,128,128]{2,1,0:T(8,128)(2,1)} %copy.87) | copy-start | bytes 12582916
  184.5 6.2 %copy-start.9 = (bf16[128,16,3,128]{3,2,1,0:T(4,128)(2,1)S(1)}, bf16[128,16,3,128]{3,2,1,0:T(4,128)(2,1)}, u32[]{:S(2)}) copy-start(bf16[128,16,3,128]{3,2,1,0:T(4,128)(2,1)} %reshape_squeeze.9) | copy-start | bytes 4718596
  200.7 6.2 %copy-start.8 = (bf16[128,16,3,128]{3,2,1,0:T(4,128)(2,1)S(1)}, bf16[128,16,3,128]{3,2,1,0:T(4,128)(2,1)}, u32[]{:S(2)}) copy-start(bf16[128,16,3,128]{3,2,1,0:T(4,128)(2,1)} %reshape_squeeze.8) | copy-start | bytes 4718596
  289.2 8.1 %copy-start.12 = (f32[1,2048,384]{2,1,0:T(8,128)S(1)}, f32[1,2048,384]{2,1,0:T(8,128)}, u32[]{:S(2)}) copy-start(f32[1,2048,384]{2,1,0:T(8,128)} %add.74) | copy-start | bytes 9437188
  297.3 74.8 %all-reduce.3.cloned.1.call-start = ((), (), s32[]{:S(2)}) async-start(), calls=%async_computation.2 | async-start | bytes 131072 | tf_op jit(solution)/shard_map/psum | solution.py:110
  297.3 6.5 %copy-start.17 = (bf16[2,2048,384]{2,1,0:T(8,128)(2,1)S(1)}, bf16[2,2048,384]{2,1,0:T(8,128)(2,1)}, u32[]{:S(2)}) copy-start(bf16[2,2048,384]{2,1,0:T(8,128)(2,1)} %param.9) | copy-start | bytes 9437188
  297.3 6.5 %copy-start.18 = (bf16[2,2048,384]{2,1,0:T(8,128)(2,1)S(1)}, bf16[2,2048,384]{2,1,0:T(8,128)(2,1)}, u32[]{:S(2)}) copy-start(bf16[2,2048,384]{2,1,0:T(8,128)(2,1)} %param.6) | copy-start | bytes 9437188
  301.9 4.3 %copy-start.14 = (f32[1,2048,384]{2,1,0:T(8,128)S(1)}, f32[1,2048,384]{2,1,0:T(8,128)}, u32[]{:S(2)}) copy-start(f32[1,2048,384]{2,1,0:T(8,128)} %add.70) | copy-start | bytes 9437188
  (5 other events, 13.4 us)
Sparse Core Ops, SparseCore 0:
  297.4 20.1 reduce-scatter.1
  320.6 51.4 all-reduce.2
where the time goes:
time: 386 us; the launch traced here: 381 us
  local copies, waits for them, and re-layouts  182 us (47%)
  waiting for transfers between devices  58.4 us (15%)
  matrix products  55.8 us (14%)
  other arithmetic  47.4 us (12%)
  between operations  14.6 us (4%)
  blocking collectives  14.4 us (4%)
  starting transfers between devices  7.83 us (2%)
    psum x1, waiting for transfers between devices, shards(): whole_grad = lax.psum(table_grad, ('dp', 'ctx'))  52.5 us
    dot_general x4, matrix products, band_outer(): jnp.einsum('rmbi,rmbj->rij', left_rows.reshape(shape_four), right_rows.re...  21.9 us
    dot_general x4, matrix products, band_apply(): jnp.einsum('rmbj,rij->rmbi', blocked, matrix, preferred_element_type=jnp....  21.6 us
    add x4, local copies, waits for them, and re-layouts, shards(): mixed_rows + band_apply(lower_band, previous, block_rows, groups_here)  19.9 us
    add x4, local copies, waits for them, and re-layouts, shards(): upward + band_adjoint(lower_band, following, block_rows, groups_here)  19.8 us
    add x1, other arithmetic, shards(): outer_total + jnp.concatenate([band_outer(backward_w, previous, block_row...  17.8 us
    unnamed x51, local copies, waits for them, and re-layouts  17.8 us
    add x1, local copies, waits for them, and re-layouts, shards(): outer_total + jnp.concatenate([band_outer(backward_w, previous, block_row...  17.7 us
  transfers between devices with their start and end apart: 4, of which 2 were waited for; matrix products, arithmetic and copies ran while one was open for 32% of the time, Pallas kernels for 0%

commit v1 on v0

--- a/solution.py
+++ b/solution.py
@@ -107,7 +107,7 @@
     table_grad = (
         jnp.dot(selector.astype(wide).T, run_grad, precision=lax.Precision.HIGHEST) * scale_by
     )
-    whole_grad = lax.psum(table_grad, ("dp", "ctx"))
+    whole_grad = jnp.sum(lax.all_gather(table_grad, ("dp", "ctx")), axis=0)
     grad_filters = lax.psum_scatter(whole_grad, "tp", scatter_dimension=0, tiled=True)
     return (gated_out, grad_queries, grad_keys, grad_values, grad_filters)
 

time: 386 us -> 342 us (0.89)
  waiting for transfers between devices: 58.4 us -> 14.4 us
  matrix products: 55.8 us -> 49.8 us
  local copies, waits for them, and re-layouts: 182 us -> 186 us
    psum x1 -> x0, waiting for transfers between devices: 52.5 us -> none  [shards(): whole_grad = lax.psum(table_grad, ('dp', 'ctx'))]
    reduce_scatter x1, waiting for transfers between devices: 5.94 us -> 14.3 us  [shards(): lax.psum_scatter(whole_grad, 'tp', scatter_dimension=0, tiled=True)]
    add x1, other arithmetic: 17.8 us -> 13.9 us  [shards(): outer_total + jnp.concatenate([band_outer(backward_w, previous, block_row...]
    unnamed x51 -> x48, local copies, waits for them, and re-layouts: 17.8 us -> 18.1 us
  transfers between devices with their start and end apart: 4 -> 4, of which waited for: 2 -> 1; matrix products, arithmetic and copies ran while one was open for 32% -> 41% of each run, Pallas kernels for 0% -> 0%
where the time goes in v1:
time: 342 us; the launch traced here: 337 us
  local copies, waits for them, and re-layouts  186 us (54%)
  other arithmetic  50 us (15%)
  matrix products  49.8 us (15%)
  between operations  14.6 us (4%)
  blocking collectives  14.4 us (4%)
  waiting for transfers between devices  14.4 us (4%)
  starting transfers between devices  8.05 us (2%)
    dot_general x4, matrix products, band_outer(): jnp.einsum('rmbi,rmbj->rij', left_rows.reshape(shape_four), right_rows.re...  21.3 us
    add x4, local copies, waits for them, and re-layouts, shards(): mixed_rows + band_apply(lower_band, previous, block_rows, groups_here)  19.8 us
    add x4, local copies, waits for them, and re-layouts, shards(): upward + band_adjoint(lower_band, following, block_rows, groups_here)  19.5 us
    dot_general x4, matrix products, band_apply(): jnp.einsum('rmbj,rij->rmbi', blocked, matrix, preferred_element_type=jnp....  19.1 us
    unnamed x48, local copies, waits for them, and re-layouts  18.1 us
    add x1, local copies, waits for them, and re-layouts, shards(): outer_total + jnp.concatenate([band_outer(backward_w, previous, block_row...  17.7 us
    reshape x1, local copies, waits for them, and re-layouts, shards(): flattened.reshape(groups_here, block_rows, 2 * block_rows + 1)  17.5 us
    another operation x2, local copies, waits for them, and re-layouts, shards(): jnp.tile(template, (1, block_rows))[:, :2 * block_rows * block_rows]  17.4 us
  transfers between devices with their start and end apart: 4, of which 1 were waited for; matrix products, arithmetic and copies ran while one was open for 41% of the time, Pallas kernels for 0%

profile of v1, /device:TPU:0, one launch (start us, length us, event | category | flops | bytes accessed | tf_op | source)
XLA Modules:
  0.0 336.8 jit_solution(5719579797917263187)
XLA Ops:
  15.2 6.5 %collective-permute-start = (bf16[2,2048,128]{2,1,0:T(8,128)(2,1)}, bf16[2,2048,128]{2,1,0:T(8,128)(2,1)}, u32[]{:S(2)}, u32[]{:S(2)}) collective-permute-start(bf16[2,2048,128]{2,1,0:T(8,128)(2,1)} %slice.112), channel_id=1, source_target_pairs={{0,4},{4,8},{8,12},{1,5},{5,9},{9,13},{2,6},{6,10},{10,14},{3,7},{... | collective-permute-start | bytes 3145736 | tf_op jit(solution)/shard_map/ppermute | solution.py:13
  25.3 14.4 %all_gather.9 = bf16[512,128]{1,0:T(8,128)(2,1)S(1)} all-gather(bf16[128,128]{1,0:T(8,128)(2,1)S(1)} %convert_element_type.96), channel_id=1, replica_groups=mesh['dp'=2,'ctx'=4,'tp'=4] {'tp'}, dimensions={0}, use_global_device_ids=true | all-gather | bytes 163840 | tf_op jit(solution)/shard_map/all_gather | solution.py:51
  44.8 12.9 %tile.10 = bf16[128,32896]{0,1:T(8,128)(2,1)} reshape(bf16[128,128,257]{0,2,1:T(8,128)(2,1)} %tile.4) | data formatting | bytes 16842752 | tf_op jit(solution)/shard_map/tile | solution.py:65
  64.9 6.8 %copy.88 = bf16[128,128,128]{2,1,0:T(8,128)(2,1)} copy(bf16[128,128,128]{0,2,1:T(8,128)(2,1)} %get-tuple-element.6) | data formatting | bytes 8388608
  75.6 6.7 %copy.87 = bf16[128,128,128]{2,1,0:T(8,128)(2,1)} copy(bf16[128,128,128]{0,2,1:T(8,128)(2,1)} %get-tuple-element.5) | data formatting | bytes 8388608
  82.3 5.1 %reshape_squeeze.21 = bf16[128,16,3,128]{3,2,1,0:T(4,128)(2,1)} reshape(bf16[1,2048,384]{2,1,0:T(8,128)(2,1)} %get-tuple-element.14) | data formatting | bytes 3145728 | tf_op jit(solution)/shard_map/reshape;squeeze | solution.py:27
  93.6 5.1 %reshape_squeeze.9 = bf16[128,16,3,128]{3,2,1,0:T(4,128)(2,1)} reshape(bf16[1,2048,384]{2,1,0:T(8,128)(2,1)} %get-tuple-element.22) | data formatting | bytes 3145728 | tf_op jit(solution)/shard_map/reshape;squeeze | solution.py:18
  103.9 6.9 %convolution_bitcast_fusion = f32[128,128,128]{1,2,0:T(8,128)} fusion(bf16[128,16,3,128]{3,2,1,0:T(4,128)(2,1)} %reshape_squeeze.9, bf16[128,16,3,128]{3,2,1,0:T(4,128)(2,1)} %reshape_squeeze.21), kind=kOutput, calls=%fused_computation.19 | convolution fusion | flops 201326592 | bytes 11534336 | tf_op jit(solution)/shard_map/rmbi,rmbj->rij/dot_general | solution.py:37
  118.6 5.2 %reshape.133 = bf16[128,16,3,128]{3,2,1,0:T(4,128)(2,1)} reshape(bf16[2048,384]{1,0:T(8,128)(2,1)} %get-tuple-element.29) | data formatting | bytes 3145728 | tf_op jit(solution)/shard_map/reshape | solution.py:27
  128.4 5.6 %reshape.132 = bf16[128,16,3,128]{3,2,1,0:T(4,128)(2,1)} reshape(bf16[2048,384]{1,0:T(8,128)(2,1)} %get-tuple-element.28) | data formatting | bytes 3145728 | tf_op jit(solution)/shard_map/reshape | solution.py:18
  134.1 6.9 %convolution_bitcast_fusion.1 = f32[128,128,128]{1,2,0:T(8,128)} fusion(bf16[128,16,3,128]{3,2,1,0:T(4,128)(2,1)} %reshape.132, bf16[128,16,3,128]{3,2,1,0:T(4,128)(2,1)} %reshape_squeeze.21), kind=kOutput, calls=%fused_computation.20 | convolution fusion | flops 201326592 | bytes 11534336 | tf_op jit(solution)/shard_map/rmbi,rmbj->rij/dot_general | solution.py:37
  152.9 6.0 %add.72 = f32[1,2048,384]{2,1,0:T(8,128)} reshape(f32[128,16,3,128]{3,2,1,0:T(4,128)} %copy.67) | data formatting | bytes 6291456 | tf_op jit(solution)/shard_map/add | solution.py:88
  158.9 5.3 %reshape.134 = bf16[128,16,3,128]{3,2,1,0:T(4,128)(2,1)} reshape(bf16[2048,384]{1,0:T(8,128)(2,1)} %get-tuple-element.30) | data formatting | bytes 3145728 | tf_op jit(solution)/shard_map/reshape | solution.py:27
  174.0 6.0 %add.74 = f32[1,2048,384]{2,1,0:T(8,128)} reshape(f32[128,16,3,128]{3,2,1,0:T(4,128)} %copy.70) | data formatting | bytes 6291456 | tf_op jit(solution)/shard_map/add | solution.py:88
  188.0 13.9 %maximum_add_fusion = f32[128,128,256]{1,2,0:T(8,128)} fusion(f32[128,128,128]{1,2,0:T(8,128)} %convolution_bitcast_fusion.2, f32[128,128,128]{1,2,0:T(8,128)S(1)} %convolution_bitcast_fusion.3, f32[128,128,128]{1,2,0:T(8,128)} %convolution_bitcast_fusion, f32[128,128,128]{1,2,0:T(8,128)} %convolution_bitcast_fusion.1), kind=kLoop, calls=%fused_computation | loop fusion | flops 12582912 | bytes 50331648 | tf_op jit(solution)/shard_map/add | solution.py:91
  201.9 17.7 %copy.79 = f32[128,128,256]{0,2,1:T(8,128)} copy(f32[128,128,256]{1,2,0:T(8,128)} %maximum_add_fusion) | data formatting | bytes 33554432 | tf_op jit(solution)/shard_map/add | solution.py:91
  219.6 13.3 %pad.4 = f32[128,32896]{0,1:T(8,128)} pad(f32[128,32768]{0,1:T(8,128)} %bitcast.68, f32[]{:T(128)} %constant.4.clone.1), padding=0_0x0_128 | pad | bytes 33619972 | tf_op jit(solution)/shard_map/jit(_pad)/pad | solution.py:103
  232.9 17.5 %reshape.135 = f32[128,128,257]{0,2,1:T(8,128)} reshape(f32[128,32896]{0,1:T(8,128)} %pad.4) | data formatting | bytes 33685504 | tf_op jit(solution)/shard_map/reshape | solution.py:104
  250.3 6.9 %reduce_sum.18 = f32[128,257]{0,1:T(8,128)S(1)} reduce(f32[128,128,257]{0,2,1:T(8,128)} %reshape.135, f32[]{:T(128)} %constant.4.clone.1), dimensions={1}, to_apply=%region_0.1 | reduce | flops 4177792 | bytes 16974340 | tf_op jit(solution)/shard_map/reduce_sum | solution.py:104
  258.6 6.2 %fusion.19 = f32[128,16,3,128]{3,1,2,0:T(8,128)S(1)} fusion(f32[128,16,3,128]{3,1,2,0:T(8,128)} %fusion.4, bf16[128,128,128]{2,1,0:T(8,128)(2,1)} %copy.87, bf16[128,16,3,128]{3,2,1,0:T(4,128)(2,1)S(1)} %copy-done.8), kind=kOutput, calls=%fused_computation.36 | convolution fusion | flops 202113024 | bytes 12058624 | tf_op jit(solution)/shard_map/rmbj,rij->rmbi/dot_general | solution.py:21
  268.5 6.2 %add.70 = f32[1,2048,384]{2,1,0:T(8,128)} reshape(f32[128,16,3,128]{3,2,1,0:T(4,128)} %copy.64) | data formatting | bytes 6291456 | tf_op jit(solution)/shard_map/add | solution.py:84
  274.7 5.3 %fusion.6 = f32[128,16,3,128]{3,1,2,0:T(8,128)S(1)} fusion(bf16[128,128,128]{2,1,0:T(8,128)(2,1)} %copy.88, bf16[128,16,3,128]{3,2,1,0:T(4,128)(2,1)S(1)} %copy-done.9), kind=kOutput, calls=%fused_computation.9 | convolution fusion | flops 201326592 | bytes 8912896 | tf_op jit(solution)/shard_map/rmbj,rij->rmbi/dot_general | solution.py:21
  286.8 6.2 %add.68 = f32[1,2048,384]{2,1,0:T(8,128)} reshape(f32[128,16,3,128]{3,2,1,0:T(4,128)} %copy.61) | data formatting | bytes 6291456 | tf_op jit(solution)/shard_map/add | solution.py:84
  315.4 14.3 %reduce-scatter.2.cloned.1.call-done = f32[128,128]{1,0:T(8,128)} async-done(((f32[512,128]{1,0:T(8,128)}), f32[128,128]{1,0:T(8,128)}) %reduce-scatter.2.cloned.1.call-update) | async-done | bytes 65552 | tf_op jit(solution)/shard_map/reduce_scatter | solution.py:111
  (107 shorter events, 115.4 us)
Async XLA Ops:
  7.2 299.9 %all-gather.3.cloned.1.call-start = ((), (), s32[]{:S(2)}) async-start(), calls=%async_computation.2 | async-start | bytes 2359296 | tf_op jit(solution)/shard_map/all_gather | solution.py:110
  7.2 6.1 %copy-start.14 = (bf16[2,2048,384]{2,1,0:T(8,128)(2,1)S(1)}, bf16[2,2048,384]{2,1,0:T(8,128)(2,1)}, u32[]{:S(2)}) copy-start(bf16[2,2048,384]{2,1,0:T(8,128)(2,1)} %param.8) | copy-start | bytes 9437188
  7.2 6.1 %copy-start.15 = (bf16[2,2048,384]{2,1,0:T(8,128)(2,1)S(1)}, bf16[2,2048,384]{2,1,0:T(8,128)(2,1)}, u32[]{:S(2)}) copy-start(bf16[2,2048,384]{2,1,0:T(8,128)(2,1)} %param.7) | copy-start | bytes 9437188
  12.0 103.4 %collective-permute-start.1 = (bf16[2,2048,128]{2,1,0:T(8,128)(2,1)}, bf16[2,2048,128]{2,1,0:T(8,128)(2,1)}, u32[]{:S(2)}, u32[]{:S(2)}) collective-permute-start(bf16[2,2048,128]{2,1,0:T(8,128)(2,1)} %slice.121), channel_id=1, source_target_pairs={{4,0},{8,4},{12,8},{5,1},{9,5},{13,9},{6,2},{10,6},{14,10},{7,3},{... | collective-permute-start | bytes 3145736 | tf_op jit(solution)/shard_map/ppermute | solution.py:13
  14.1 9.8 %copy-start.5 = (bf16[2,2048,384]{2,1,0:T(8,128)(2,1)}, bf16[2,2048,384]{2,1,0:T(8,128)(2,1)S(1)}, u32[]{:S(2)}) copy-start(bf16[2,2048,384]{2,1,0:T(8,128)(2,1)S(1)} %multiply_convert_fusion.1) | copy-start | bytes 9437188
  15.2 108.6 %collective-permute-start = (bf16[2,2048,128]{2,1,0:T(8,128)(2,1)}, bf16[2,2048,128]{2,1,0:T(8,128)(2,1)}, u32[]{:S(2)}, u32[]{:S(2)}) collective-permute-start(bf16[2,2048,128]{2,1,0:T(8,128)(2,1)} %slice.112), channel_id=1, source_target_pairs={{0,4},{4,8},{8,12},{1,5},{5,9},{9,13},{2,6},{6,10},{10,14},{3,7},{... | collective-permute-start | bytes 3145736 | tf_op jit(solution)/shard_map/ppermute | solution.py:13
  103.9 6.9 %copy-start.6 = (bf16[128,16,3,128]{3,2,1,0:T(4,128)(2,1)S(1)}, bf16[128,16,3,128]{3,2,1,0:T(4,128)(2,1)}, u32[]{:S(2)}) copy-start(bf16[128,16,3,128]{3,2,1,0:T(4,128)(2,1)} %reshape_squeeze.8) | copy-start | bytes 4718596
  110.8 5.9 %copy-start.19 = (bf16[2048,256]{1,0:T(8,128)(2,1)S(1)}, bf16[2048,256]{1,0:T(8,128)(2,1)}, u32[]{:S(2)}) copy-start(bf16[2048,256]{1,0:T(8,128)(2,1)} %slice.124) | copy-start | bytes 3145732
  118.6 6.5 %copy-start.20 = (bf16[2048,256]{1,0:T(8,128)(2,1)S(1)}, bf16[2048,256]{1,0:T(8,128)(2,1)}, u32[]{:S(2)}) copy-start(bf16[2048,256]{1,0:T(8,128)(2,1)} %slice.114) | copy-start | bytes 3145732
  134.1 7.0 %copy-start.3 = (bf16[128,128,128]{2,1,0:T(8,128)(2,1)S(1)}, bf16[128,128,128]{2,1,0:T(8,128)(2,1)}, u32[]{:S(2)}) copy-start(bf16[128,128,128]{2,1,0:T(8,128)(2,1)} %copy.88) | copy-start | bytes 12582916
  134.1 7.0 %copy-start.10 = (bf16[128,16,3,128]{3,2,1,0:T(4,128)(2,1)S(1)}, bf16[128,16,3,128]{3,2,1,0:T(4,128)(2,1)}, u32[]{:S(2)}) copy-start(bf16[128,16,3,128]{3,2,1,0:T(4,128)(2,1)} %reshape.132) | copy-start | bytes 4718596
  141.0 4.7 %copy-start.18 = (bf16[128,16,3,128]{3,2,1,0:T(4,128)(2,1)S(1)}, bf16[128,16,3,128]{3,2,1,0:T(4,128)(2,1)}, u32[]{:S(2)}) copy-start(bf16[128,16,3,128]{3,2,1,0:T(4,128)(2,1)} %reshape.133) | copy-start | bytes 4718596
  164.2 4.2 %copy-start.1 = (bf16[128,128,128]{2,1,0:T(8,128)(2,1)S(1)}, bf16[128,128,128]{2,1,0:T(8,128)(2,1)}, u32[]{:S(2)}) copy-start(bf16[128,128,128]{2,1,0:T(8,128)(2,1)} %copy.87) | copy-start | bytes 12582916
  164.2 4.7 %copy-start.4 = (bf16[128,16,3,128]{3,2,1,0:T(4,128)(2,1)S(1)}, bf16[128,16,3,128]{3,2,1,0:T(4,128)(2,1)}, u32[]{:S(2)}) copy-start(bf16[128,16,3,128]{3,2,1,0:T(4,128)(2,1)} %reshape_squeeze.21) | copy-start | bytes 4718596
  250.3 8.3 %copy-start.8 = (bf16[128,16,3,128]{3,2,1,0:T(4,128)(2,1)S(1)}, bf16[128,16,3,128]{3,2,1,0:T(4,128)(2,1)}, u32[]{:S(2)}) copy-start(bf16[128,16,3,128]{3,2,1,0:T(4,128)(2,1)} %reshape_squeeze.9) | copy-start | bytes 4718596
  258.4 71.4 %reduce-scatter.2.cloned.1.call-start = ((), (), s32[]{:S(2)}) async-start(), calls=%async_computation.1 | async-start | bytes 327680 | tf_op jit(solution)/shard_map/reduce_scatter | solution.py:111
  268.5 6.2 %copy-start.9 = (bf16[128,16,3,128]{3,2,1,0:T(4,128)(2,1)S(1)}, bf16[128,16,3,128]{3,2,1,0:T(4,128)(2,1)}, u32[]{:S(2)}) copy-start(bf16[128,16,3,128]{3,2,1,0:T(4,128)(2,1)} %reshape.131) | copy-start | bytes 4718596
  274.7 5.3 %copy-start.2 = (bf16[128,128,128]{2,1,0:T(8,128)(2,1)S(1)}, bf16[128,128,128]{2,1,0:T(8,128)(2,1)}, u32[]{:S(2)}) copy-start(bf16[128,128,128]{2,1,0:T(8,128)(2,1)} %copy.87) | copy-start | bytes 12582916
  274.7 5.3 %copy-start.7 = (bf16[128,16,3,128]{3,2,1,0:T(4,128)(2,1)S(1)}, bf16[128,16,3,128]{3,2,1,0:T(4,128)(2,1)}, u32[]{:S(2)}) copy-start(bf16[128,16,3,128]{3,2,1,0:T(4,128)(2,1)} %reshape_squeeze.8) | copy-start | bytes 4718596
  286.8 6.2 %copy-start.11 = (f32[1,2048,384]{2,1,0:T(8,128)S(1)}, f32[1,2048,384]{2,1,0:T(8,128)}, u32[]{:S(2)}) copy-start(f32[1,2048,384]{2,1,0:T(8,128)} %add.72) | copy-start | bytes 9437188
  297.3 4.1 %copy-start.16 = (bf16[2,2048,384]{2,1,0:T(8,128)(2,1)S(1)}, bf16[2,2048,384]{2,1,0:T(8,128)(2,1)}, u32[]{:S(2)}) copy-start(bf16[2,2048,384]{2,1,0:T(8,128)(2,1)} %param.9) | copy-start | bytes 9437188
  297.3 5.1 %copy-start.17 = (bf16[2,2048,384]{2,1,0:T(8,128)(2,1)S(1)}, bf16[2,2048,384]{2,1,0:T(8,128)(2,1)}, u32[]{:S(2)}) copy-start(bf16[2,2048,384]{2,1,0:T(8,128)(2,1)} %param.6) | copy-start | bytes 9437188
  299.3 4.2 %copy-start.12 = (f32[1,2048,384]{2,1,0:T(8,128)S(1)}, f32[1,2048,384]{2,1,0:T(8,128)}, u32[]{:S(2)}) copy-start(f32[1,2048,384]{2,1,0:T(8,128)} %add.70) | copy-start | bytes 9437188
  299.3 5.1 %copy-start.13 = (f32[1,2048,384]{2,1,0:T(8,128)S(1)}, f32[1,2048,384]{2,1,0:T(8,128)}, u32[]{:S(2)}) copy-start(f32[1,2048,384]{2,1,0:T(8,128)} %add.68) | copy-start | bytes 9437188
  (4 other events, 8.0 us)
Sparse Core Ops, SparseCore 0:
  258.5 27.8 all-gather.2
  309.6 20.0 reduce-scatter.1
